TPU v7x, 32 devices: a whole 2x2x4 slice. The times are simulated.
32 devices in a mesh: clip: 8 (over y, x, core), tm: 4 (over z).
Axes of the slice: x: 2, y: 2, z: 4, core: 2. Of those that a mesh axis runs over, the one named last changes fastest.
Arguments:
- features: bfloat16 [16, 4, 64, 1024], P('clip', 'tm'), may hold values from -6 to 6
- flow_forward: int32 [16, 4, 2, 16], P('clip', 'tm'), may hold values from -4 to 4
- flow_backward: int32 [16, 4, 2, 16], P('clip', 'tm'), may hold values from -4 to 4
- w_forward_in: bfloat16 [64, 1152], replicated, may hold values from -0.1875 to 0.1875
- b_forward_in: float32 [64], replicated, may hold values from -3 to 3
- w_forward_out: bfloat16 [64, 576], replicated, may hold values from -0.25 to 0.25
- b_forward_out: float32 [64], replicated, may hold values from -3 to 3
- w_backward_in: bfloat16 [64, 1152], replicated, may hold values from -0.1875 to 0.1875
- b_backward_in: float32 [64], replicated, may hold values from -3 to 3
- w_backward_out: bfloat16 [64, 576], replicated, may hold values from -0.25 to 0.25
- b_backward_out: float32 [64], replicated, may hold values from -3 to 3
- w_merge: bfloat16 [64, 1152], replicated, may hold values from -0.1875 to 0.1875
- b_merge: float32 [64], replicated, may hold values from -3 to 3
- w_head: bfloat16 [48, 64], replicated, may hold values from -0.75 to 0.75
- b_head: float32 [48], replicated, may hold values from -3 to 3
- target: bfloat16 [16, 4, 48, 1024], P('clip', 'tm'), may hold values from -24 to 24
Outputs:
- restored: bfloat16 [16, 4, 48, 1024], P('clip', 'tm')
- grad_merge: float32 [64, 1152], replicated
- grad_head: float32 [48, 64], replicated
- loss: float32 [], replicated
All inputs are finite; a program needn't handle non-finite values.
Results may differ from a plain program's by a relative error of at most 0.0085.
Values may be sent and summed in bfloat16 or wider, within the bound.
A program may use at most 64 MiB of HBM per device.

v0:
```python
import jax
import jax.numpy as jnp
from jax import lax
from jax.sharding import PartitionSpec as P

CHANNELS = 64
SUBPIX = 48
PATCH_ROWS = 32
PATCH_COLS = 32
PIXELS = 1024
flow_reach = 4
tile_rows = 8
block_side = 8
clip_limit = 128.0
leak_slope = 0.1


def shifted(value, axis, steps):
    count = lax.axis_size(axis)
    first, last = (max(0, -steps), min(count, count - steps))
    return lax.ppermute(value, axis, [(source, source + steps) for source in range(first, last)])


def flat_taps(source, height, width):
    pixels = height * width
    padded = jnp.pad(source, ((0, 0), (width + 1, width + 1)))
    col_pos = lax.broadcasted_iota(jnp.int32, (1, pixels), 1) % width
    layers = []
    for row_off in (-1, 0, 1):
        for col_off in (-1, 0, 1):
            start = width + 1 + row_off * width + col_off
            piece = padded[:, start : start + pixels]
            if col_off != 0:
                valid = (col_pos + col_off >= 0) & (col_pos + col_off < width)
                piece = jnp.where(valid, piece, jnp.zeros_like(piece))
            layers.append(piece)
    return layers


def apply_taps(weight, groups):
    total_in = sum((group[0].shape[0] for group in groups))
    result = None
    for tap_index in range(9):
        offset = tap_index * total_in
        for group in groups:
            width_in = group[tap_index].shape[0]
            block = weight[:, offset : offset + width_in]
            term = jnp.dot(block, group[tap_index], preferred_element_type=jnp.float32)
            result = term if result is None else result + term
            offset = offset + width_in
    return result


def warp_state(hidden_state, flow_map, height, width):
    padded = jnp.pad(hidden_state, ((0, 0), (flow_reach * width, flow_reach * width)))
    grid_shape = (height // block_side, width // block_side)
    shift_rows = jnp.repeat(
        jnp.repeat(flow_map[0].reshape(grid_shape), block_side, 0), block_side, 1
    )
    shift_cols = jnp.repeat(
        jnp.repeat(flow_map[1].reshape(grid_shape), block_side, 0), block_side, 1
    )
    row_pos = lax.broadcasted_iota(jnp.int32, (height, width), 0)
    col_pos = lax.broadcasted_iota(jnp.int32, (height, width), 1)
    source_col = col_pos + shift_cols
    inside = (source_col >= 0) & (source_col < width)
    window_rows = tile_rows + 2 * flow_reach
    window_cell = lax.broadcasted_iota(jnp.int32, (window_rows * width, tile_rows * width), 0)
    pieces = []
    for tile_index in range(height // tile_rows):
        row_start = tile_index * tile_rows
        window = padded[:, row_start * width : (row_start + window_rows) * width]
        local_row = (
            row_pos[row_start : row_start + tile_rows]
            + shift_rows[row_start : row_start + tile_rows]
            - row_start
            + flow_reach
        )
        target_cell = local_row * width + source_col[row_start : row_start + tile_rows]
        target_cell = jnp.where(inside[row_start : row_start + tile_rows], target_cell, -1).reshape(
            -1
        )
        one_hot = (window_cell == target_cell[None, :]).astype(jnp.bfloat16)
        pieces.append(jnp.dot(window, one_hot, preferred_element_type=jnp.float32))
    return jnp.concatenate(pieces, axis=1).astype(jnp.bfloat16)


def propagate(prior_state, feature, flow_map, weights, height, width):
    w_first, b_first, w_second, b_second = weights
    warped = warp_state(prior_state, flow_map, height, width)
    first_out = (
        apply_taps(w_first, (flat_taps(warped, height, width), flat_taps(feature, height, width)))
        + b_first[:, None]
    )
    first_out = jax.nn.leaky_relu(first_out, leak_slope).astype(jnp.bfloat16)
    second_out = apply_taps(w_second, (flat_taps(first_out, height, width),)) + b_second[:, None]
    return (warped.astype(jnp.float32) + second_out).astype(jnp.bfloat16)


def merge_and_grade(fwd_state, bwd_state, target_frame, merge_weights, height, width, loss_scale):
    w_merge, b_merge, w_head, b_head = merge_weights
    groups = (flat_taps(fwd_state, height, width), flat_taps(bwd_state, height, width))
    mixed_pre = apply_taps(w_merge, groups) + b_merge[:, None]
    sigmoid_part = jax.nn.sigmoid(mixed_pre)
    active = (mixed_pre * sigmoid_part).astype(jnp.bfloat16)
    output = jnp.dot(w_head, active, preferred_element_type=jnp.float32) + b_head[:, None]
    misfit = output - target_frame.astype(jnp.float32)
    loss_part = 0.5 * loss_scale * jnp.sum(misfit * misfit)
    errors = (misfit * loss_scale).astype(jnp.bfloat16)
    grad_head = lax.dot_general(
        errors, active, (((1,), (1,)), ((), ())), preferred_element_type=jnp.float32
    )
    back_grad = lax.dot_general(
        w_head, errors, (((0,), (0,)), ((), ())), preferred_element_type=jnp.float32
    )
    silu_slope = sigmoid_part * (1.0 + mixed_pre * (1.0 - sigmoid_part))
    d_mixed = (back_grad * silu_slope).astype(jnp.bfloat16)
    blocks = []
    for tap_index in range(9):
        for group in groups:
            blocks.append(
                lax.dot_general(
                    d_mixed,
                    group[tap_index],
                    (((1,), (1,)), ((), ())),
                    preferred_element_type=jnp.float32,
                )
            )
    grad_merge = jnp.concatenate(blocks, axis=1)
    return (output.astype(jnp.bfloat16), grad_merge, grad_head, loss_part)


def on_device(
    features,
    flow_forward,
    flow_backward,
    w_forward_in,
    b_forward_in,
    w_forward_out,
    b_forward_out,
    w_backward_in,
    b_backward_in,
    w_backward_out,
    b_backward_out,
    w_merge,
    b_merge,
    w_head,
    b_head,
    target,
):
    fwd_weights = (w_forward_in, b_forward_in, w_forward_out, b_forward_out)
    bwd_weights = (w_backward_in, b_backward_in, w_backward_out, b_backward_out)
    merge_weights = (w_merge, b_merge, w_head, b_head)
    micro_clips = features.shape[0]
    sections = lax.axis_size("tm")
    section_index = lax.axis_index("tm")
    turns = micro_clips + sections - 1
    frame_feats = features[:, 0]
    fwd_flows = flow_forward[:, 0]
    bwd_flows = flow_backward[:, 0]
    blank_states = jnp.zeros((micro_clips, CHANNELS, PIXELS), jnp.bfloat16)
    seed_state = jnp.zeros((CHANNELS, PIXELS), jnp.bfloat16)
    bwd_offset = sections - 1 - section_index

    def advance(turn_index, offset, incoming, states, flows, weights):
        member = turn_index - offset
        active_flag = (member >= 0) & (member < micro_clips)
        member = jnp.clip(member, 0, micro_clips - 1)
        feature = lax.dynamic_index_in_dim(frame_feats, member, 0, keepdims=False)
        flow_map = lax.dynamic_index_in_dim(flows, member, 0, keepdims=False)
        produced = propagate(incoming, feature, flow_map, weights, PATCH_ROWS, PATCH_COLS)
        former = lax.dynamic_index_in_dim(states, member, 0, keepdims=False)
        states = lax.dynamic_update_index_in_dim(
            states, jnp.where(active_flag, produced, former), member, 0
        )
        return (produced, states)

    def forward_turn(turn_index, carried):
        produced, states = advance(
            turn_index, section_index, carried[0], carried[1], fwd_flows, fwd_weights
        )
        return (shifted(produced, "tm", 1), states)

    def backward_turn(turn_index, carried):
        produced, states = advance(
            turn_index, bwd_offset, carried[0], carried[1], bwd_flows, bwd_weights
        )
        return (shifted(produced, "tm", -1), states)

    fwd_states = lax.fori_loop(0, turns, forward_turn, (seed_state, blank_states))[1]
    bwd_states = lax.fori_loop(0, turns, backward_turn, (seed_state, blank_states))[1]
    loss_scale = 1.0 / (micro_clips * lax.axis_size("clip") * sections)

    def grade_member(totals, inputs):
        frame_out, grad_merge, grad_head, loss_part = merge_and_grade(
            inputs[0], inputs[1], inputs[2], merge_weights, PATCH_ROWS, PATCH_COLS, loss_scale
        )
        return ((totals[0] + grad_merge, totals[1] + grad_head, totals[2] + loss_part), frame_out)

    initial = (
        jnp.zeros((CHANNELS, 18 * CHANNELS), jnp.float32),
        jnp.zeros((SUBPIX, CHANNELS), jnp.float32),
        jnp.zeros((), jnp.float32),
    )
    totals, frames_out = lax.scan(grade_member, initial, (fwd_states, bwd_states, target[:, 0]))
    restored = frames_out[:, None]
    grad_merge, grad_head, loss_total = lax.psum((totals[0], totals[1], totals[2]), ("clip", "tm"))
    squares = jnp.sum(grad_merge * grad_merge) + jnp.sum(grad_head * grad_head)
    factor = jnp.minimum(1.0, clip_limit / jnp.sqrt(squares + 1e-06))
    return (restored, grad_merge * factor, grad_head * factor, loss_total)


def solution(mesh):
    in_specs = (
        P("clip", "tm", None, None),
        P("clip", "tm", None, None),
        P("clip", "tm", None, None),
        P(),
        P(),
        P(),
        P(),
        P(),
        P(),
        P(),
        P(),
        P(),
        P(),
        P(),
        P(),
        P("clip", "tm", None, None),
    )
    out_specs = (P("clip", "tm", None, None), P(), P(), P())
    return jax.shard_map(
        on_device, mesh=mesh, in_specs=in_specs, out_specs=out_specs, check_vma=False
    )
```

profile of v0, /device:TPU:8, one launch (start us, length us, event | category | flops | bytes accessed | tf_op | source)
XLA Modules:
  0.0 339.6 jit_solution(3447712072973825057)
XLA Ops:
  7.4 0.8 copy-done.4
  8.2 85.5 %while.57 = (s32[]{:T(128)}, bf16[64,1024]{1,0:T(8,128)(2,1)S(1)}, bf16[2,64,1024]{2,1,0:T(8,128)(2,1)S(1)}, s32[]{:T(128)}, s32[2,2,16]{2,1,0:T(2,128)S(1)}, /*...) while((s32[]{:T(128)}, bf16[64,1024]{1,0:T(8,128)(2,1)S(1)}, ...), condition=%wide.region_1.2_spmd, body=%wide.region_0.1_spmd.sunk | while | flops 299203584 | bytes 19935880 | solution.py:190
  18.4 3.5 %collective-permute-start = (bf16[64,1024]{1,0:T(8,128)(2,1)S(1)}, bf16[64,1024]{1,0:T(8,128)(2,1)S(1)}, u32[]{:S(2)}, u32[]{:S(2)}) collective-permute-start(bf16[64,1024]{1,0:T(8,128)(2,1)S(1)} %get-tuple-element.1151), channel_id=1, source_target_pairs={{0,1},{1,2},{2,3},{4,5},{5,6},{6,7},{8,9},{9,10},{10,11},{12,13},{... | collective-permute-start | bytes 393224 | tf_op jit(solution)/shard_map/while/body/eval_jaxpr/ppermute | solution.py:21
  21.9 3.6 %collective-permute-done = bf16[64,1024]{1,0:T(8,128)(2,1)S(1)} collective-permute-done((bf16[64,1024]{1,0:T(8,128)(2,1)S(1)}, bf16[64,1024]{1,0:T(8,128)(2,1)S(1)}, u32[]{:S(2)}, u32[]{:S(2)}) %collective-permute-start) | collective-permute-done | bytes 131104 | tf_op jit(solution)/shard_map/while/body/eval_jaxpr/ppermute | solution.py:21
  35.7 3.5 %collective-permute-start = (bf16[64,1024]{1,0:T(8,128)(2,1)S(1)}, bf16[64,1024]{1,0:T(8,128)(2,1)S(1)}, u32[]{:S(2)}, u32[]{:S(2)}) collective-permute-start(bf16[64,1024]{1,0:T(8,128)(2,1)S(1)} %get-tuple-element.1151), channel_id=1, source_target_pairs={{0,1},{1,2},{2,3},{4,5},{5,6},{6,7},{8,9},{9,10},{10,11},{12,13},{... | collective-permute-start | bytes 393224 | tf_op jit(solution)/shard_map/while/body/eval_jaxpr/ppermute | solution.py:21
  39.2 3.4 collective-permute-done
  52.8 3.5 %collective-permute-start = (bf16[64,1024]{1,0:T(8,128)(2,1)S(1)}, bf16[64,1024]{1,0:T(8,128)(2,1)S(1)}, u32[]{:S(2)}, u32[]{:S(2)}) collective-permute-start(bf16[64,1024]{1,0:T(8,128)(2,1)S(1)} %get-tuple-element.1151), channel_id=1, source_target_pairs={{0,1},{1,2},{2,3},{4,5},{5,6},{6,7},{8,9},{9,10},{10,11},{12,13},{... | collective-permute-start | bytes 393224 | tf_op jit(solution)/shard_map/while/body/eval_jaxpr/ppermute | solution.py:21
  56.3 3.4 collective-permute-done
  69.8 3.5 %collective-permute-start = (bf16[64,1024]{1,0:T(8,128)(2,1)S(1)}, bf16[64,1024]{1,0:T(8,128)(2,1)S(1)}, u32[]{:S(2)}, u32[]{:S(2)}) collective-permute-start(bf16[64,1024]{1,0:T(8,128)(2,1)S(1)} %get-tuple-element.1151), channel_id=1, source_target_pairs={{0,1},{1,2},{2,3},{4,5},{5,6},{6,7},{8,9},{9,10},{10,11},{12,13},{... | collective-permute-start | bytes 393224 | tf_op jit(solution)/shard_map/while/body/eval_jaxpr/ppermute | solution.py:21
  73.3 3.4 collective-permute-done
  86.8 3.5 %collective-permute-start = (bf16[64,1024]{1,0:T(8,128)(2,1)S(1)}, bf16[64,1024]{1,0:T(8,128)(2,1)S(1)}, u32[]{:S(2)}, u32[]{:S(2)}) collective-permute-start(bf16[64,1024]{1,0:T(8,128)(2,1)S(1)} %get-tuple-element.1151), channel_id=1, source_target_pairs={{0,1},{1,2},{2,3},{4,5},{5,6},{6,7},{8,9},{9,10},{10,11},{12,13},{... | collective-permute-start | bytes 393224 | tf_op jit(solution)/shard_map/while/body/eval_jaxpr/ppermute | solution.py:21
  90.3 3.4 collective-permute-done
  93.8 0.8 copy-done.1
  94.7 82.1 %while.58 = (s32[]{:T(128)}, bf16[64,1024]{1,0:T(8,128)(2,1)S(1)}, bf16[2,64,1024]{2,1,0:T(8,128)(2,1)S(1)}, s32[]{:T(128)}, s32[2,2,16]{2,1,0:T(2,128)S(1)}, /*...) while((s32[]{:T(128)}, bf16[64,1024]{1,0:T(8,128)(2,1)S(1)}, ...), condition=%wide.region_3.4_spmd, body=%wide.region_2.3_spmd.sunk | while | flops 299203584 | bytes 19640940 | solution.py:191
  104.3 1.9 collective-permute-start.1
  106.2 4.9 %collective-permute-done.1 = bf16[64,1024]{1,0:T(8,128)(2,1)S(1)} collective-permute-done((bf16[64,1024]{1,0:T(8,128)(2,1)S(1)}, bf16[64,1024]{1,0:T(8,128)(2,1)S(1)}, u32[]{:S(2)}, u32[]{:S(2)}) %collective-permute-start.1) | collective-permute-done | bytes 131104 | tf_op jit(solution)/shard_map/while/body/eval_jaxpr/ppermute | solution.py:21
  120.7 1.9 collective-permute-start.1
  122.7 4.9 %collective-permute-done.1 = bf16[64,1024]{1,0:T(8,128)(2,1)S(1)} collective-permute-done((bf16[64,1024]{1,0:T(8,128)(2,1)S(1)}, bf16[64,1024]{1,0:T(8,128)(2,1)S(1)}, u32[]{:S(2)}, u32[]{:S(2)}) %collective-permute-start.1) | collective-permute-done | bytes 131104 | tf_op jit(solution)/shard_map/while/body/eval_jaxpr/ppermute | solution.py:21
  137.2 1.9 collective-permute-start.1
  139.1 4.9 %collective-permute-done.1 = bf16[64,1024]{1,0:T(8,128)(2,1)S(1)} collective-permute-done((bf16[64,1024]{1,0:T(8,128)(2,1)S(1)}, bf16[64,1024]{1,0:T(8,128)(2,1)S(1)}, u32[]{:S(2)}, u32[]{:S(2)}) %collective-permute-start.1) | collective-permute-done | bytes 131104 | tf_op jit(solution)/shard_map/while/body/eval_jaxpr/ppermute | solution.py:21
  153.6 1.9 collective-permute-start.1
  155.5 4.9 %collective-permute-done.1 = bf16[64,1024]{1,0:T(8,128)(2,1)S(1)} collective-permute-done((bf16[64,1024]{1,0:T(8,128)(2,1)S(1)}, bf16[64,1024]{1,0:T(8,128)(2,1)S(1)}, u32[]{:S(2)}, u32[]{:S(2)}) %collective-permute-start.1) | collective-permute-done | bytes 131104 | tf_op jit(solution)/shard_map/while/body/eval_jaxpr/ppermute | solution.py:21
  170.0 1.9 collective-permute-start.1
  171.9 4.9 %collective-permute-done.1 = bf16[64,1024]{1,0:T(8,128)(2,1)S(1)} collective-permute-done((bf16[64,1024]{1,0:T(8,128)(2,1)S(1)}, bf16[64,1024]{1,0:T(8,128)(2,1)S(1)}, u32[]{:S(2)}, u32[]{:S(2)}) %collective-permute-start.1) | collective-permute-done | bytes 131104 | tf_op jit(solution)/shard_map/while/body/eval_jaxpr/ppermute | solution.py:21
  177.5 22.3 %while.59 = (s32[]{:T(128)}, f32[64,1152]{1,0:T(8,128)S(1)}, f32[48,64]{1,0:T(8,128)S(1)}, f32[]{:T(128)}, bf16[2,48,1024]{2,1,0:T(8,128)(2,1)S(1)}, /*index=5*/...) while((s32[]{:T(128)}, f32[64,1152]{1,0:T(8,128)S(1)}, ...), condition=%wide.region_6.7_spmd.clone, body=%wide.region_4.6_spmd.clone.sunk | while | flops 325101568 | bytes 20380548 | solution.py:205
  182.1 0.8 multiply_reduce_fusion.4
  193.3 0.8 multiply_reduce_fusion.4
  199.9 0.7 copy-done.3
  200.6 40.0 %all-reduce.10 = (f32[48,64]{1,0:T(8,128)S(1)}, f32[]{:T(128)}) all-reduce(f32[48,64]{1,0:T(8,128)S(1)} %get-tuple-element.806, f32[]{:T(128)} %get-tuple-element.807), channel_id=1, replica_groups=mesh['clip'=8,'tm'=4] {'clip','tm'}, use_global_device_ids=true, to_apply=%region_9.10 | all-reduce | flops 3073 | bytes 24584 | tf_op jit(solution)/shard_map/psum | solution.py:207
  241.3 87.1 %all-reduce.13.cloned.1.call-done = f32[64,1152]{1,0:T(8,128)} async-done(((f32[64,1152]{1,0:T(8,128)}), f32[64,1152]{1,0:T(8,128)}) %all-reduce.13.cloned.1.call-update) | async-done | bytes 294928 | tf_op jit(solution)/shard_map/psum | solution.py:207
  328.4 1.7 multiply_reduce_fusion.1
  332.0 0.7 broadcast_multiply_fusion
  (762 shorter events, 117.0 us)
Async XLA Ops:
  7.2 1.0 copy-start.4
  7.2 321.2 %all-reduce.13.cloned.1.call-start = ((), (), s32[]{:S(2)}) async-start(), calls=%async_computation | async-start | bytes 589824 | tf_op jit(solution)/shard_map/psum | solution.py:207
  7.3 0.9 copy-start
  7.3 0.9 copy-start.11
  7.3 0.9 copy-start.13
  7.3 0.9 copy-start.16
  15.3 0.9 copy-start.5
  18.4 7.1 %collective-permute-start = (bf16[64,1024]{1,0:T(8,128)(2,1)S(1)}, bf16[64,1024]{1,0:T(8,128)(2,1)S(1)}, u32[]{:S(2)}, u32[]{:S(2)}) collective-permute-start(bf16[64,1024]{1,0:T(8,128)(2,1)S(1)} %get-tuple-element.1151), channel_id=1, source_target_pairs={{0,1},{1,2},{2,3},{4,5},{5,6},{6,7},{8,9},{9,10},{10,11},{12,13},{... | collective-permute-start | bytes 393224 | tf_op jit(solution)/shard_map/while/body/eval_jaxpr/ppermute | solution.py:21
  32.6 0.9 copy-start.5
  35.7 6.9 %collective-permute-start = (bf16[64,1024]{1,0:T(8,128)(2,1)S(1)}, bf16[64,1024]{1,0:T(8,128)(2,1)S(1)}, u32[]{:S(2)}, u32[]{:S(2)}) collective-permute-start(bf16[64,1024]{1,0:T(8,128)(2,1)S(1)} %get-tuple-element.1151), channel_id=1, source_target_pairs={{0,1},{1,2},{2,3},{4,5},{5,6},{6,7},{8,9},{9,10},{10,11},{12,13},{... | collective-permute-start | bytes 393224 | tf_op jit(solution)/shard_map/while/body/eval_jaxpr/ppermute | solution.py:21
  49.6 0.9 copy-start.5
  52.8 6.9 %collective-permute-start = (bf16[64,1024]{1,0:T(8,128)(2,1)S(1)}, bf16[64,1024]{1,0:T(8,128)(2,1)S(1)}, u32[]{:S(2)}, u32[]{:S(2)}) collective-permute-start(bf16[64,1024]{1,0:T(8,128)(2,1)S(1)} %get-tuple-element.1151), channel_id=1, source_target_pairs={{0,1},{1,2},{2,3},{4,5},{5,6},{6,7},{8,9},{9,10},{10,11},{12,13},{... | collective-permute-start | bytes 393224 | tf_op jit(solution)/shard_map/while/body/eval_jaxpr/ppermute | solution.py:21
  66.7 0.9 copy-start.5
  69.8 6.9 %collective-permute-start = (bf16[64,1024]{1,0:T(8,128)(2,1)S(1)}, bf16[64,1024]{1,0:T(8,128)(2,1)S(1)}, u32[]{:S(2)}, u32[]{:S(2)}) collective-permute-start(bf16[64,1024]{1,0:T(8,128)(2,1)S(1)} %get-tuple-element.1151), channel_id=1, source_target_pairs={{0,1},{1,2},{2,3},{4,5},{5,6},{6,7},{8,9},{9,10},{10,11},{12,13},{... | collective-permute-start | bytes 393224 | tf_op jit(solution)/shard_map/while/body/eval_jaxpr/ppermute | solution.py:21
  83.7 0.9 copy-start.5
  86.8 6.9 %collective-permute-start = (bf16[64,1024]{1,0:T(8,128)(2,1)S(1)}, bf16[64,1024]{1,0:T(8,128)(2,1)S(1)}, u32[]{:S(2)}, u32[]{:S(2)}) collective-permute-start(bf16[64,1024]{1,0:T(8,128)(2,1)S(1)} %get-tuple-element.1151), channel_id=1, source_target_pairs={{0,1},{1,2},{2,3},{4,5},{5,6},{6,7},{8,9},{9,10},{10,11},{12,13},{... | collective-permute-start | bytes 393224 | tf_op jit(solution)/shard_map/while/body/eval_jaxpr/ppermute | solution.py:21
  93.7 0.9 copy-start.1
  93.7 1.0 copy-start.6
  93.7 0.9 copy-start.12
  93.7 0.9 copy-start.14
  93.8 0.9 copy-start.17
  94.7 82.2 %copy-start.2 = (bf16[64,1152]{1,0:T(8,128)(2,1)S(1)}, bf16[64,1152]{1,0:T(8,128)(2,1)}, u32[]{:S(2)}) copy-start(bf16[64,1152]{1,0:T(8,128)(2,1)} %param.33) | copy-start | bytes 442372
  94.7 82.2 %copy-start.7 = (bf16[2,1,48,1024]{3,2,1,0:T(8,128)(2,1)S(1)}, bf16[2,1,48,1024]{3,2,1,0:T(8,128)(2,1)}, u32[]{:S(2)}) copy-start(bf16[2,1,48,1024]{3,2,1,0:T(8,128)(2,1)} %param.37) | copy-start | bytes 589828
  94.7 82.2 %copy-start.9 = (bf16[48,64]{1,0:T(8,128)(2,1)S(1)}, bf16[48,64]{1,0:T(8,128)(2,1)}, u32[]{:S(2)}) copy-start(bf16[48,64]{1,0:T(8,128)(2,1)} %param.35) | copy-start | bytes 18436
  104.3 6.9 %collective-permute-start.1 = (bf16[64,1024]{1,0:T(8,128)(2,1)S(1)}, bf16[64,1024]{1,0:T(8,128)(2,1)S(1)}, u32[]{:S(2)}, u32[]{:S(2)}) collective-permute-start(bf16[64,1024]{1,0:T(8,128)(2,1)S(1)} %get-tuple-element.1171), channel_id=1, source_target_pairs={{1,0},{2,1},{3,2},{5,4},{6,5},{7,6},{9,8},{10,9},{11,10},{13,12},{... | collective-permute-start | bytes 393224 | tf_op jit(solution)/shard_map/while/body/eval_jaxpr/ppermute | solution.py:21
  120.7 6.9 %collective-permute-start.1 = (bf16[64,1024]{1,0:T(8,128)(2,1)S(1)}, bf16[64,1024]{1,0:T(8,128)(2,1)S(1)}, u32[]{:S(2)}, u32[]{:S(2)}) collective-permute-start(bf16[64,1024]{1,0:T(8,128)(2,1)S(1)} %get-tuple-element.1171), channel_id=1, source_target_pairs={{1,0},{2,1},{3,2},{5,4},{6,5},{7,6},{9,8},{10,9},{11,10},{13,12},{... | collective-permute-start | bytes 393224 | tf_op jit(solution)/shard_map/while/body/eval_jaxpr/ppermute | solution.py:21
  137.2 6.9 %collective-permute-start.1 = (bf16[64,1024]{1,0:T(8,128)(2,1)S(1)}, bf16[64,1024]{1,0:T(8,128)(2,1)S(1)}, u32[]{:S(2)}, u32[]{:S(2)}) collective-permute-start(bf16[64,1024]{1,0:T(8,128)(2,1)S(1)} %get-tuple-element.1171), channel_id=1, source_target_pairs={{1,0},{2,1},{3,2},{5,4},{6,5},{7,6},{9,8},{10,9},{11,10},{13,12},{... | collective-permute-start | bytes 393224 | tf_op jit(solution)/shard_map/while/body/eval_jaxpr/ppermute | solution.py:21
  153.6 6.9 %collective-permute-start.1 = (bf16[64,1024]{1,0:T(8,128)(2,1)S(1)}, bf16[64,1024]{1,0:T(8,128)(2,1)S(1)}, u32[]{:S(2)}, u32[]{:S(2)}) collective-permute-start(bf16[64,1024]{1,0:T(8,128)(2,1)S(1)} %get-tuple-element.1171), channel_id=1, source_target_pairs={{1,0},{2,1},{3,2},{5,4},{6,5},{7,6},{9,8},{10,9},{11,10},{13,12},{... | collective-permute-start | bytes 393224 | tf_op jit(solution)/shard_map/while/body/eval_jaxpr/ppermute | solution.py:21
  170.0 6.9 %collective-permute-start.1 = (bf16[64,1024]{1,0:T(8,128)(2,1)S(1)}, bf16[64,1024]{1,0:T(8,128)(2,1)S(1)}, u32[]{:S(2)}, u32[]{:S(2)}) collective-permute-start(bf16[64,1024]{1,0:T(8,128)(2,1)S(1)} %get-tuple-element.1171), channel_id=1, source_target_pairs={{1,0},{2,1},{3,2},{5,4},{6,5},{7,6},{9,8},{10,9},{11,10},{13,12},{... | collective-permute-start | bytes 393224 | tf_op jit(solution)/shard_map/while/body/eval_jaxpr/ppermute | solution.py:21
  199.9 0.7 copy-start.3
  199.9 130.2 %copy-start.15 = (bf16[2,48,1024]{2,1,0:T(8,128)(2,1)}, bf16[2,48,1024]{2,1,0:T(8,128)(2,1)S(1)}, u32[]{:S(2)}) copy-start(bf16[2,48,1024]{2,1,0:T(8,128)(2,1)S(1)} %get-tuple-element.804) | copy-start | bytes 589828
  328.4 3.6 %copy-start.8 = (f32[64,1152]{1,0:T(8,128)S(1)}, f32[64,1152]{1,0:T(8,128)}, u32[]{:S(2)}) copy-start(f32[64,1152]{1,0:T(8,128)} %all-reduce.13.cloned.1.call-done) | copy-start | bytes 884740
  (2 other events, 1.3 us)
Sparse Core Ops, SparseCore 0:
  200.7 127.6 all-reduce.12
where the time goes:
time: 340 us
  waiting for transfers between devices  129 us (38%)
  matrix products  94.4 us (28%)
  blocking collectives  40 us (12%)
  starting transfers between devices  27.1 us (8%)
  local copies, waits for them, and re-layouts  23.4 us (7%)
  between operations  15.5 us (5%)
  other arithmetic  5.51 us (2%)
  loops' own time  4.82 us (1%)
    psum x1, waiting for transfers between devices, on_device(): lax.psum((totals[0], totals[1], totals[2]), ('clip', 'tm'))  87.1 us
    dot_general x306, matrix products, apply_taps(): term = jnp.dot(block, group[tap_index], preferred_element_type=jnp.float32)  74 us
    ppermute x10, waiting for transfers between devices, shifted(): lax.ppermute(value, axis, [(source, source + steps) for source in range(f...  41.7 us
    psum x1, blocking collectives, on_device(): lax.psum((totals[0], totals[1], totals[2]), ('clip', 'tm'))  40 us
    ppermute x10, starting transfers between devices, shifted(): lax.ppermute(value, axis, [(source, source + steps) for source in range(f...  27.1 us
    dot_general x40, matrix products, warp_state(): pieces.append(jnp.dot(window, one_hot, preferred_element_type=jnp.float32))  9.38 us
    dot_general x36, matrix products, merge_and_grade(): lax.dot_general(d_mixed, group[tap_index], (((1,), (1,)), ((), ())), pref...  8.63 us
  transfers between devices with their start and end apart: 11, of which 11 were waited for; matrix products, arithmetic and copies ran while one was open for 0% of the time, Pallas kernels for 0%

commit v1 on v0

--- a/solution.py
+++ b/solution.py
@@ -204,7 +204,9 @@
     )
     totals, frames_out = lax.scan(grade_member, initial, (fwd_states, bwd_states, target[:, 0]))
     restored = frames_out[:, None]
-    grad_merge, grad_head, loss_total = lax.psum((totals[0], totals[1], totals[2]), ("clip", "tm"))
+    grad_merge, grad_head, loss_total = lax.psum(
+        lax.psum((totals[0], totals[1], totals[2]), "tm"), "clip"
+    )
     squares = jnp.sum(grad_merge * grad_merge) + jnp.sum(grad_head * grad_head)
     factor = jnp.minimum(1.0, clip_limit / jnp.sqrt(squares + 1e-06))
     return (restored, grad_merge * factor, grad_head * factor, loss_total)

time: 340 us -> 306 us (0.900)
  waiting for transfers between devices: 129 us -> 94.6 us
    psum x1 -> x2, waiting for transfers between devices: 87.1 us -> 52.8 us  [the longest x1 35.9 us: on_device(): lax.psum((totals[0], totals[1], totals[2]), 'tm')]
    psum x1 -> x2, blocking collectives: 40 us -> 38.5 us  [the longest x1 22.4 us: on_device(): lax.psum(lax.psum((totals[0], totals[1], totals[2]), 'tm'), 'clip')]
  transfers between devices with their start and end apart: 11 -> 12, of which waited for: 11 -> 12; matrix products, arithmetic and copies ran while one was open for 0% -> 0% of each run, Pallas kernels for 0% -> 0%
where the time goes in v1:
time: 306 us; the launch traced here: 304 us
  waiting for transfers between devices  94.6 us (31%)
  matrix products  94.4 us (31%)
  blocking collectives  38.5 us (13%)
  starting transfers between devices  27.1 us (9%)
  local copies, waits for them, and re-layouts  23.4 us (8%)
  between operations  15.6 us (5%)
  other arithmetic  5.48 us (2%)
  loops' own time  4.83 us (2%)
    dot_general x306, matrix products, apply_taps(): term = jnp.dot(block, group[tap_index], preferred_element_type=jnp.float32)  74 us
    ppermute x10, waiting for transfers between devices, shifted(): lax.ppermute(value, axis, [(source, source + steps) for source in range(f...  41.7 us
    psum x1, waiting for transfers between devices, on_device(): lax.psum((totals[0], totals[1], totals[2]), 'tm')  35.9 us
    ppermute x10, starting transfers between devices, shifted(): lax.ppermute(value, axis, [(source, source + steps) for source in range(f...  27.1 us
    psum x1, blocking collectives, on_device(): lax.psum(lax.psum((totals[0], totals[1], totals[2]), 'tm'), 'clip')  22.4 us
    psum x1, waiting for transfers between devices, on_device(): lax.psum(lax.psum((totals[0], totals[1], totals[2]), 'tm'), 'clip')  16.9 us
    psum x1, blocking collectives, on_device(): lax.psum((totals[0], totals[1], totals[2]), 'tm')  16 us
    dot_general x40, matrix products, warp_state(): pieces.append(jnp.dot(window, one_hot, preferred_element_type=jnp.float32))  9.38 us
  transfers between devices with their start and end apart: 12, of which 12 were waited for; matrix products, arithmetic and copies ran while one was open for 0% of the time, Pallas kernels for 0%

profile of v1, /device:TPU:8, one launch (start us, length us, event | category | flops | bytes accessed | tf_op | source)
XLA Modules:
  0.0 303.9 jit_solution(6906959869907186397)
XLA Ops:
  7.4 0.8 copy-done.4
  8.2 85.5 %while.57 = (s32[]{:T(128)}, bf16[64,1024]{1,0:T(8,128)(2,1)S(1)}, bf16[2,64,1024]{2,1,0:T(8,128)(2,1)S(1)}, s32[]{:T(128)}, s32[2,2,16]{2,1,0:T(2,128)S(1)}, /*...) while((s32[]{:T(128)}, bf16[64,1024]{1,0:T(8,128)(2,1)S(1)}, ...), condition=%wide.region_1.2_spmd, body=%wide.region_0.1_spmd.sunk | while | flops 299203584 | bytes 19935880 | solution.py:190
  18.4 3.5 %collective-permute-start = (bf16[64,1024]{1,0:T(8,128)(2,1)S(1)}, bf16[64,1024]{1,0:T(8,128)(2,1)S(1)}, u32[]{:S(2)}, u32[]{:S(2)}) collective-permute-start(bf16[64,1024]{1,0:T(8,128)(2,1)S(1)} %get-tuple-element.1153), channel_id=1, source_target_pairs={{0,1},{1,2},{2,3},{4,5},{5,6},{6,7},{8,9},{9,10},{10,11},{12,13},{... | collective-permute-start | bytes 393224 | tf_op jit(solution)/shard_map/while/body/eval_jaxpr/ppermute | solution.py:21
  21.9 3.6 %collective-permute-done = bf16[64,1024]{1,0:T(8,128)(2,1)S(1)} collective-permute-done((bf16[64,1024]{1,0:T(8,128)(2,1)S(1)}, bf16[64,1024]{1,0:T(8,128)(2,1)S(1)}, u32[]{:S(2)}, u32[]{:S(2)}) %collective-permute-start) | collective-permute-done | bytes 131104 | tf_op jit(solution)/shard_map/while/body/eval_jaxpr/ppermute | solution.py:21
  35.7 3.5 %collective-permute-start = (bf16[64,1024]{1,0:T(8,128)(2,1)S(1)}, bf16[64,1024]{1,0:T(8,128)(2,1)S(1)}, u32[]{:S(2)}, u32[]{:S(2)}) collective-permute-start(bf16[64,1024]{1,0:T(8,128)(2,1)S(1)} %get-tuple-element.1153), channel_id=1, source_target_pairs={{0,1},{1,2},{2,3},{4,5},{5,6},{6,7},{8,9},{9,10},{10,11},{12,13},{... | collective-permute-start | bytes 393224 | tf_op jit(solution)/shard_map/while/body/eval_jaxpr/ppermute | solution.py:21
  39.2 3.4 %collective-permute-done = bf16[64,1024]{1,0:T(8,128)(2,1)S(1)} collective-permute-done((bf16[64,1024]{1,0:T(8,128)(2,1)S(1)}, bf16[64,1024]{1,0:T(8,128)(2,1)S(1)}, u32[]{:S(2)}, u32[]{:S(2)}) %collective-permute-start) | collective-permute-done | bytes 131104 | tf_op jit(solution)/shard_map/while/body/eval_jaxpr/ppermute | solution.py:21
  52.8 3.5 %collective-permute-start = (bf16[64,1024]{1,0:T(8,128)(2,1)S(1)}, bf16[64,1024]{1,0:T(8,128)(2,1)S(1)}, u32[]{:S(2)}, u32[]{:S(2)}) collective-permute-start(bf16[64,1024]{1,0:T(8,128)(2,1)S(1)} %get-tuple-element.1153), channel_id=1, source_target_pairs={{0,1},{1,2},{2,3},{4,5},{5,6},{6,7},{8,9},{9,10},{10,11},{12,13},{... | collective-permute-start | bytes 393224 | tf_op jit(solution)/shard_map/while/body/eval_jaxpr/ppermute | solution.py:21
  56.3 3.4 %collective-permute-done = bf16[64,1024]{1,0:T(8,128)(2,1)S(1)} collective-permute-done((bf16[64,1024]{1,0:T(8,128)(2,1)S(1)}, bf16[64,1024]{1,0:T(8,128)(2,1)S(1)}, u32[]{:S(2)}, u32[]{:S(2)}) %collective-permute-start) | collective-permute-done | bytes 131104 | tf_op jit(solution)/shard_map/while/body/eval_jaxpr/ppermute | solution.py:21
  69.8 3.5 %collective-permute-start = (bf16[64,1024]{1,0:T(8,128)(2,1)S(1)}, bf16[64,1024]{1,0:T(8,128)(2,1)S(1)}, u32[]{:S(2)}, u32[]{:S(2)}) collective-permute-start(bf16[64,1024]{1,0:T(8,128)(2,1)S(1)} %get-tuple-element.1153), channel_id=1, source_target_pairs={{0,1},{1,2},{2,3},{4,5},{5,6},{6,7},{8,9},{9,10},{10,11},{12,13},{... | collective-permute-start | bytes 393224 | tf_op jit(solution)/shard_map/while/body/eval_jaxpr/ppermute | solution.py:21
  73.3 3.4 %collective-permute-done = bf16[64,1024]{1,0:T(8,128)(2,1)S(1)} collective-permute-done((bf16[64,1024]{1,0:T(8,128)(2,1)S(1)}, bf16[64,1024]{1,0:T(8,128)(2,1)S(1)}, u32[]{:S(2)}, u32[]{:S(2)}) %collective-permute-start) | collective-permute-done | bytes 131104 | tf_op jit(solution)/shard_map/while/body/eval_jaxpr/ppermute | solution.py:21
  86.8 3.5 %collective-permute-start = (bf16[64,1024]{1,0:T(8,128)(2,1)S(1)}, bf16[64,1024]{1,0:T(8,128)(2,1)S(1)}, u32[]{:S(2)}, u32[]{:S(2)}) collective-permute-start(bf16[64,1024]{1,0:T(8,128)(2,1)S(1)} %get-tuple-element.1153), channel_id=1, source_target_pairs={{0,1},{1,2},{2,3},{4,5},{5,6},{6,7},{8,9},{9,10},{10,11},{12,13},{... | collective-permute-start | bytes 393224 | tf_op jit(solution)/shard_map/while/body/eval_jaxpr/ppermute | solution.py:21
  90.3 3.4 %collective-permute-done = bf16[64,1024]{1,0:T(8,128)(2,1)S(1)} collective-permute-done((bf16[64,1024]{1,0:T(8,128)(2,1)S(1)}, bf16[64,1024]{1,0:T(8,128)(2,1)S(1)}, u32[]{:S(2)}, u32[]{:S(2)}) %collective-permute-start) | collective-permute-done | bytes 131104 | tf_op jit(solution)/shard_map/while/body/eval_jaxpr/ppermute | solution.py:21
  93.8 0.8 copy-done.1
  94.7 82.1 %while.58 = (s32[]{:T(128)}, bf16[64,1024]{1,0:T(8,128)(2,1)S(1)}, bf16[2,64,1024]{2,1,0:T(8,128)(2,1)S(1)}, s32[]{:T(128)}, s32[2,2,16]{2,1,0:T(2,128)S(1)}, /*...) while((s32[]{:T(128)}, bf16[64,1024]{1,0:T(8,128)(2,1)S(1)}, ...), condition=%wide.region_3.4_spmd, body=%wide.region_2.3_spmd.sunk | while | flops 299203584 | bytes 19640940 | solution.py:191
  104.3 1.9 collective-permute-start.1
  106.2 4.9 %collective-permute-done.1 = bf16[64,1024]{1,0:T(8,128)(2,1)S(1)} collective-permute-done((bf16[64,1024]{1,0:T(8,128)(2,1)S(1)}, bf16[64,1024]{1,0:T(8,128)(2,1)S(1)}, u32[]{:S(2)}, u32[]{:S(2)}) %collective-permute-start.1) | collective-permute-done | bytes 131104 | tf_op jit(solution)/shard_map/while/body/eval_jaxpr/ppermute | solution.py:21
  120.7 1.9 collective-permute-start.1
  122.7 4.9 %collective-permute-done.1 = bf16[64,1024]{1,0:T(8,128)(2,1)S(1)} collective-permute-done((bf16[64,1024]{1,0:T(8,128)(2,1)S(1)}, bf16[64,1024]{1,0:T(8,128)(2,1)S(1)}, u32[]{:S(2)}, u32[]{:S(2)}) %collective-permute-start.1) | collective-permute-done | bytes 131104 | tf_op jit(solution)/shard_map/while/body/eval_jaxpr/ppermute | solution.py:21
  137.2 1.9 collective-permute-start.1
  139.1 4.9 %collective-permute-done.1 = bf16[64,1024]{1,0:T(8,128)(2,1)S(1)} collective-permute-done((bf16[64,1024]{1,0:T(8,128)(2,1)S(1)}, bf16[64,1024]{1,0:T(8,128)(2,1)S(1)}, u32[]{:S(2)}, u32[]{:S(2)}) %collective-permute-start.1) | collective-permute-done | bytes 131104 | tf_op jit(solution)/shard_map/while/body/eval_jaxpr/ppermute | solution.py:21
  153.6 1.9 collective-permute-start.1
  155.5 4.9 %collective-permute-done.1 = bf16[64,1024]{1,0:T(8,128)(2,1)S(1)} collective-permute-done((bf16[64,1024]{1,0:T(8,128)(2,1)S(1)}, bf16[64,1024]{1,0:T(8,128)(2,1)S(1)}, u32[]{:S(2)}, u32[]{:S(2)}) %collective-permute-start.1) | collective-permute-done | bytes 131104 | tf_op jit(solution)/shard_map/while/body/eval_jaxpr/ppermute | solution.py:21
  170.0 1.9 collective-permute-start.1
  171.9 4.9 %collective-permute-done.1 = bf16[64,1024]{1,0:T(8,128)(2,1)S(1)} collective-permute-done((bf16[64,1024]{1,0:T(8,128)(2,1)S(1)}, bf16[64,1024]{1,0:T(8,128)(2,1)S(1)}, u32[]{:S(2)}, u32[]{:S(2)}) %collective-permute-start.1) | collective-permute-done | bytes 131104 | tf_op jit(solution)/shard_map/while/body/eval_jaxpr/ppermute | solution.py:21
  177.5 22.3 %while.59 = (s32[]{:T(128)}, f32[64,1152]{1,0:T(8,128)S(1)}, f32[48,64]{1,0:T(8,128)S(1)}, f32[]{:T(128)}, bf16[2,48,1024]{2,1,0:T(8,128)(2,1)S(1)}, /*index=5*/...) while((s32[]{:T(128)}, f32[64,1152]{1,0:T(8,128)S(1)}, ...), condition=%wide.region_6.7_spmd.clone, body=%wide.region_4.6_spmd.clone.sunk | while | flops 325101568 | bytes 20380548 | solution.py:205
  182.1 0.8 multiply_reduce_fusion.4
  193.3 0.8 multiply_reduce_fusion.4
  200.7 35.9 %all-reduce.15.cloned.1.call-done = f32[64,1152]{1,0:T(8,128)} async-done(((f32[64,1152]{1,0:T(8,128)}), f32[64,1152]{1,0:T(8,128)}) %all-reduce.15.cloned.1.call-update) | async-done | bytes 294928 | tf_op jit(solution)/shard_map/psum | solution.py:208
  236.6 16.0 %all-reduce.11 = (f32[48,64]{1,0:T(8,128)S(1)}, f32[]{:T(128)}) all-reduce(f32[48,64]{1,0:T(8,128)S(1)} %get-tuple-element.806, f32[]{:T(128)} %get-tuple-element.807), channel_id=1, replica_groups=mesh['clip'=8,'tm'=4] {'tm'}, use_global_device_ids=true, to_apply=%region_10.11 | all-reduce | flops 3073 | bytes 24584 | tf_op jit(solution)/shard_map/psum | solution.py:208
  252.6 22.4 %all-reduce.10 = (f32[48,64]{1,0:T(8,128)S(1)}, f32[]{:T(128)}) all-reduce(f32[48,64]{1,0:T(8,128)S(1)} %get-tuple-element.913, f32[]{:T(128)} %get-tuple-element.914), channel_id=1, replica_groups=mesh['clip'=8,'tm'=4] {'clip'}, use_global_device_ids=true, to_apply=%region_11.12 | all-reduce | flops 3073 | bytes 24584 | tf_op jit(solution)/shard_map/psum | solution.py:207
  275.7 16.9 %all-reduce.17.cloned.1.call-done = f32[64,1152]{1,0:T(8,128)} async-done(((f32[64,1152]{1,0:T(8,128)}), f32[64,1152]{1,0:T(8,128)}) %all-reduce.17.cloned.1.call-update) | async-done | bytes 294928 | tf_op jit(solution)/shard_map/psum | solution.py:207
  292.6 1.7 multiply_reduce_fusion.1
  (766 shorter events, 118.5 us)
Async XLA Ops:
  7.2 1.0 copy-start.4
  7.2 229.4 %all-reduce.15.cloned.1.call-start = ((), (), s32[]{:S(2)}) async-start(), calls=%async_computation | async-start | bytes 589824 | tf_op jit(solution)/shard_map/psum | solution.py:208
  7.3 0.9 copy-start
  7.3 0.9 copy-start.11
  7.3 0.9 copy-start.13
  7.3 0.9 copy-start.16
  15.3 0.9 copy-start.5
  18.4 7.1 %collective-permute-start = (bf16[64,1024]{1,0:T(8,128)(2,1)S(1)}, bf16[64,1024]{1,0:T(8,128)(2,1)S(1)}, u32[]{:S(2)}, u32[]{:S(2)}) collective-permute-start(bf16[64,1024]{1,0:T(8,128)(2,1)S(1)} %get-tuple-element.1153), channel_id=1, source_target_pairs={{0,1},{1,2},{2,3},{4,5},{5,6},{6,7},{8,9},{9,10},{10,11},{12,13},{... | collective-permute-start | bytes 393224 | tf_op jit(solution)/shard_map/while/body/eval_jaxpr/ppermute | solution.py:21
  32.6 0.9 copy-start.5
  35.7 6.9 %collective-permute-start = (bf16[64,1024]{1,0:T(8,128)(2,1)S(1)}, bf16[64,1024]{1,0:T(8,128)(2,1)S(1)}, u32[]{:S(2)}, u32[]{:S(2)}) collective-permute-start(bf16[64,1024]{1,0:T(8,128)(2,1)S(1)} %get-tuple-element.1153), channel_id=1, source_target_pairs={{0,1},{1,2},{2,3},{4,5},{5,6},{6,7},{8,9},{9,10},{10,11},{12,13},{... | collective-permute-start | bytes 393224 | tf_op jit(solution)/shard_map/while/body/eval_jaxpr/ppermute | solution.py:21
  49.6 0.9 copy-start.5
  52.8 6.9 %collective-permute-start = (bf16[64,1024]{1,0:T(8,128)(2,1)S(1)}, bf16[64,1024]{1,0:T(8,128)(2,1)S(1)}, u32[]{:S(2)}, u32[]{:S(2)}) collective-permute-start(bf16[64,1024]{1,0:T(8,128)(2,1)S(1)} %get-tuple-element.1153), channel_id=1, source_target_pairs={{0,1},{1,2},{2,3},{4,5},{5,6},{6,7},{8,9},{9,10},{10,11},{12,13},{... | collective-permute-start | bytes 393224 | tf_op jit(solution)/shard_map/while/body/eval_jaxpr/ppermute | solution.py:21
  66.7 0.9 copy-start.5
  69.8 6.9 %collective-permute-start = (bf16[64,1024]{1,0:T(8,128)(2,1)S(1)}, bf16[64,1024]{1,0:T(8,128)(2,1)S(1)}, u32[]{:S(2)}, u32[]{:S(2)}) collective-permute-start(bf16[64,1024]{1,0:T(8,128)(2,1)S(1)} %get-tuple-element.1153), channel_id=1, source_target_pairs={{0,1},{1,2},{2,3},{4,5},{5,6},{6,7},{8,9},{9,10},{10,11},{12,13},{... | collective-permute-start | bytes 393224 | tf_op jit(solution)/shard_map/while/body/eval_jaxpr/ppermute | solution.py:21
  83.7 0.9 copy-start.5
  86.8 6.9 %collective-permute-start = (bf16[64,1024]{1,0:T(8,128)(2,1)S(1)}, bf16[64,1024]{1,0:T(8,128)(2,1)S(1)}, u32[]{:S(2)}, u32[]{:S(2)}) collective-permute-start(bf16[64,1024]{1,0:T(8,128)(2,1)S(1)} %get-tuple-element.1153), channel_id=1, source_target_pairs={{0,1},{1,2},{2,3},{4,5},{5,6},{6,7},{8,9},{9,10},{10,11},{12,13},{... | collective-permute-start | bytes 393224 | tf_op jit(solution)/shard_map/while/body/eval_jaxpr/ppermute | solution.py:21
  93.7 0.9 copy-start.1
  93.7 1.0 copy-start.6
  93.7 0.9 copy-start.12
  93.7 0.9 copy-start.14
  93.8 0.9 copy-start.17
  94.7 82.2 %copy-start.2 = (bf16[64,1152]{1,0:T(8,128)(2,1)S(1)}, bf16[64,1152]{1,0:T(8,128)(2,1)}, u32[]{:S(2)}) copy-start(bf16[64,1152]{1,0:T(8,128)(2,1)} %param.33) | copy-start | bytes 442372
  94.7 82.2 %copy-start.7 = (bf16[2,1,48,1024]{3,2,1,0:T(8,128)(2,1)S(1)}, bf16[2,1,48,1024]{3,2,1,0:T(8,128)(2,1)}, u32[]{:S(2)}) copy-start(bf16[2,1,48,1024]{3,2,1,0:T(8,128)(2,1)} %param.37) | copy-start | bytes 589828
  94.7 82.2 %copy-start.9 = (bf16[48,64]{1,0:T(8,128)(2,1)S(1)}, bf16[48,64]{1,0:T(8,128)(2,1)}, u32[]{:S(2)}) copy-start(bf16[48,64]{1,0:T(8,128)(2,1)} %param.35) | copy-start | bytes 18436
  104.3 6.9 %collective-permute-start.1 = (bf16[64,1024]{1,0:T(8,128)(2,1)S(1)}, bf16[64,1024]{1,0:T(8,128)(2,1)S(1)}, u32[]{:S(2)}, u32[]{:S(2)}) collective-permute-start(bf16[64,1024]{1,0:T(8,128)(2,1)S(1)} %get-tuple-element.1173), channel_id=1, source_target_pairs={{1,0},{2,1},{3,2},{5,4},{6,5},{7,6},{9,8},{10,9},{11,10},{13,12},{... | collective-permute-start | bytes 393224 | tf_op jit(solution)/shard_map/while/body/eval_jaxpr/ppermute | solution.py:21
  120.7 6.9 %collective-permute-start.1 = (bf16[64,1024]{1,0:T(8,128)(2,1)S(1)}, bf16[64,1024]{1,0:T(8,128)(2,1)S(1)}, u32[]{:S(2)}, u32[]{:S(2)}) collective-permute-start(bf16[64,1024]{1,0:T(8,128)(2,1)S(1)} %get-tuple-element.1173), channel_id=1, source_target_pairs={{1,0},{2,1},{3,2},{5,4},{6,5},{7,6},{9,8},{10,9},{11,10},{13,12},{... | collective-permute-start | bytes 393224 | tf_op jit(solution)/shard_map/while/body/eval_jaxpr/ppermute | solution.py:21
  137.2 6.9 %collective-permute-start.1 = (bf16[64,1024]{1,0:T(8,128)(2,1)S(1)}, bf16[64,1024]{1,0:T(8,128)(2,1)S(1)}, u32[]{:S(2)}, u32[]{:S(2)}) collective-permute-start(bf16[64,1024]{1,0:T(8,128)(2,1)S(1)} %get-tuple-element.1173), channel_id=1, source_target_pairs={{1,0},{2,1},{3,2},{5,4},{6,5},{7,6},{9,8},{10,9},{11,10},{13,12},{... | collective-permute-start | bytes 393224 | tf_op jit(solution)/shard_map/while/body/eval_jaxpr/ppermute | solution.py:21
  153.6 6.9 %collective-permute-start.1 = (bf16[64,1024]{1,0:T(8,128)(2,1)S(1)}, bf16[64,1024]{1,0:T(8,128)(2,1)S(1)}, u32[]{:S(2)}, u32[]{:S(2)}) collective-permute-start(bf16[64,1024]{1,0:T(8,128)(2,1)S(1)} %get-tuple-element.1173), channel_id=1, source_target_pairs={{1,0},{2,1},{3,2},{5,4},{6,5},{7,6},{9,8},{10,9},{11,10},{13,12},{... | collective-permute-start | bytes 393224 | tf_op jit(solution)/shard_map/while/body/eval_jaxpr/ppermute | solution.py:21
  170.0 6.9 %collective-permute-start.1 = (bf16[64,1024]{1,0:T(8,128)(2,1)S(1)}, bf16[64,1024]{1,0:T(8,128)(2,1)S(1)}, u32[]{:S(2)}, u32[]{:S(2)}) collective-permute-start(bf16[64,1024]{1,0:T(8,128)(2,1)S(1)} %get-tuple-element.1173), channel_id=1, source_target_pairs={{1,0},{2,1},{3,2},{5,4},{6,5},{7,6},{9,8},{10,9},{11,10},{13,12},{... | collective-permute-start | bytes 393224 | tf_op jit(solution)/shard_map/while/body/eval_jaxpr/ppermute | solution.py:21
  199.9 36.7 %copy-start.15 = (bf16[2,48,1024]{2,1,0:T(8,128)(2,1)}, bf16[2,48,1024]{2,1,0:T(8,128)(2,1)S(1)}, u32[]{:S(2)}) copy-start(bf16[2,48,1024]{2,1,0:T(8,128)(2,1)S(1)} %get-tuple-element.804) | copy-start | bytes 589828
  200.6 92.0 %all-reduce.17.cloned.1.call-start = ((), (), s32[]{:S(2)}) async-start(), calls=%async_computation.1 | async-start | bytes 589824 | tf_op jit(solution)/shard_map/psum | solution.py:207
  292.6 3.7 %copy-start.8 = (f32[64,1152]{1,0:T(8,128)S(1)}, f32[64,1152]{1,0:T(8,128)}, u32[]{:S(2)}) copy-start(f32[64,1152]{1,0:T(8,128)} %all-reduce.17.cloned.1.call-done) | copy-start | bytes 884740
  (3 other events, 2.0 us)
Sparse Core Ops, SparseCore 0:
  200.7 35.8 all-reduce.14
  239.7 52.8 all-reduce.16
